TPU v7x, 32 devices: a whole 2x2x4 slice. The times are simulated.
32 devices in a mesh: dp: 4 (over y, core), ctx: 8 (over z, x).
Axes of the slice: x: 2, y: 2, z: 4, core: 2. Of those that a mesh axis runs over, the one named last changes fastest.
Arguments:
- layer_input: bfloat16 [8, 1024, 1024], P('dp', 'ctx'), may hold values from -6 to 6
- doc_ids: int32 [8, 1024], P('dp'), may hold values from 0 to 4, as said below
- attn_gain: bfloat16 [1024], P(('dp', 'ctx')), may hold values from 0.099609375 to 1.8984375
- query_weight: bfloat16 [1024, 1024], P(('dp', 'ctx')), may hold values from -0.25 to 0.25
- key_weight: bfloat16 [1024, 1024], P(('dp', 'ctx')), may hold values from -0.1875 to 0.1875
- value_weight: bfloat16 [1024, 1024], P(('dp', 'ctx')), may hold values from -0.1875 to 0.1875
- out_weight: bfloat16 [1024, 1024], P(('dp', 'ctx')), may hold values from -1.5 to 1.5
- mlp_gain: bfloat16 [1024], P(('dp', 'ctx')), may hold values from 0.099609375 to 1.8984375
- gate_weight: bfloat16 [1024, 4096], P(('dp', 'ctx')), may hold values from -0.1875 to 0.1875
- up_weight: bfloat16 [1024, 4096], P(('dp', 'ctx')), may hold values from -0.1875 to 0.1875
- down_weight: bfloat16 [4096, 1024], P(('dp', 'ctx')), may hold values from -0.1875 to 0.1875
- out_grad: bfloat16 [8, 1024, 1024], P('dp', 'ctx'), may hold values from -6 to 6
Outputs:
- layer_output: bfloat16 [8, 1024, 1024], P('dp', 'ctx')
- input_grad: float32 [8, 1024, 1024], P('dp', 'ctx')
- attn_gain_grad: float32 [1024], P(('dp', 'ctx'))
- query_grad: float32 [1024, 1024], P(('dp', 'ctx'))
- key_grad: float32 [1024, 1024], P(('dp', 'ctx'))
- value_grad: float32 [1024, 1024], P(('dp', 'ctx'))
- out_proj_grad: float32 [1024, 1024], P(('dp', 'ctx'))
- mlp_gain_grad: float32 [1024], P(('dp', 'ctx'))
- gate_grad: float32 [1024, 4096], P(('dp', 'ctx'))
- up_grad: float32 [1024, 4096], P(('dp', 'ctx'))
- down_grad: float32 [4096, 1024], P(('dp', 'ctx'))
Inputs may be any that keep to these rules, and one draw needn't show every extreme that they name: Within each sequence doc_ids start at 0 and never fall; the rows of one value form one document of 60 to 800 rows, except the document at one end of a sequence, which may be shorter; every sequence holds one document of exactly 800 rows, at its start or at its end; in the first sequence all other documents but the one at its other end have exactly 60 rows.
All inputs are finite; a program needn't handle non-finite values.
Results may differ from a plain program's by a relative error of at most 0.015.
Values may be sent and summed in bfloat16 or wider, within the bound.
A program may use at most 256 MiB of HBM per device.

v0:
```python
import jax
import jax.numpy as jnp
from jax import lax
from jax.sharding import PartitionSpec as P

HEAD = 64
EPS = 1e-05


def product(left, right):
    return jnp.dot(left, right, preferred_element_type=jnp.float32)


def product_left(left, right):
    return lax.dot_general(
        left, right, (((0,), (0,)), ((), ())), preferred_element_type=jnp.float32
    )


def product_right(left, right):
    return lax.dot_general(
        left, right, (((1,), (1,)), ((), ())), preferred_element_type=jnp.float32
    )


def normalize(rows, gain):
    inverse = lax.rsqrt(jnp.mean(rows * rows, axis=-1, keepdims=True) + EPS)
    return (rows * inverse * gain, inverse)


def norm_back(rows, inverse, gain, upstream):
    normed = rows * inverse
    scaled = upstream * gain
    grad_rows = inverse * (scaled - normed * jnp.mean(scaled * normed, axis=-1, keepdims=True))
    return (grad_rows, jnp.sum(upstream * normed, axis=0))


def head_pair(array, start):
    piece = lax.dynamic_slice_in_dim(array, start, 2 * HEAD, 2)
    return piece.reshape(array.shape[0], array.shape[1], 2, HEAD)


def pair_scores(query, keys, allowed, start):
    scores = jnp.einsum(
        "sqhd,skhd->shqk",
        head_pair(query, start),
        head_pair(keys, start),
        preferred_element_type=jnp.float32,
    ) * HEAD ** (-0.5)
    return jnp.where(allowed[:, None], scores, -1e30)


def attend(query, keys, values, allowed):
    groups, rows, width = query.shape

    def step(index, carry):
        mixed_all, logsum = carry
        start = index * 2 * HEAD
        scores = pair_scores(query, keys, allowed, start)
        top = jnp.max(scores, axis=-1, keepdims=True)
        lifted = jnp.exp(scores - top)
        total = jnp.sum(lifted, axis=-1, keepdims=True)
        probs = (lifted / total).astype(jnp.bfloat16)
        mixed = jnp.einsum(
            "shqk,skhd->sqhd", probs, head_pair(values, start), preferred_element_type=jnp.float32
        )
        mixed_all = lax.dynamic_update_slice_in_dim(
            mixed_all, mixed.reshape(groups, rows, 2 * HEAD).astype(jnp.bfloat16), start, 2
        )
        logsum = lax.dynamic_update_slice_in_dim(
            logsum, (top + jnp.log(total))[..., 0], index * 2, 1
        )
        return (mixed_all, logsum)

    start_state = (
        jnp.zeros((groups, rows, width), jnp.bfloat16),
        jnp.zeros((groups, width // HEAD, rows), jnp.float32),
    )
    return lax.fori_loop(0, width // (2 * HEAD), step, start_state)


def attend_back(query, keys, values, allowed, logsum, grad_mixed):
    groups, rows, width = query.shape
    length = keys.shape[1]
    scale = HEAD ** (-0.5)

    def step(index, carry):
        grad_query, grad_keys, grad_values = carry
        start = index * 2 * HEAD
        scores = pair_scores(query, keys, allowed, start)
        kept = lax.dynamic_slice_in_dim(logsum, index * 2, 2, 1)
        probs = jnp.exp(scores - kept[..., None])
        upstream = head_pair(grad_mixed, start)
        grad_probs = jnp.einsum(
            "sqhd,skhd->shqk",
            upstream,
            head_pair(values, start),
            preferred_element_type=jnp.float32,
        )
        grad_scores = (
            probs * (grad_probs - jnp.sum(probs * grad_probs, axis=-1, keepdims=True))
        ).astype(jnp.bfloat16)
        part_query = (
            jnp.einsum(
                "shqk,skhd->sqhd",
                grad_scores,
                head_pair(keys, start),
                preferred_element_type=jnp.float32,
            )
            * scale
        )
        part_keys = (
            jnp.einsum(
                "shqk,sqhd->skhd",
                grad_scores,
                head_pair(query, start),
                preferred_element_type=jnp.float32,
            )
            * scale
        )
        part_values = jnp.einsum(
            "shqk,sqhd->skhd",
            probs.astype(jnp.bfloat16),
            upstream,
            preferred_element_type=jnp.float32,
        )
        grad_query = lax.dynamic_update_slice_in_dim(
            grad_query, part_query.reshape(groups, rows, 2 * HEAD), start, 2
        )
        grad_keys = lax.dynamic_update_slice_in_dim(
            grad_keys, part_keys.reshape(groups, length, 2 * HEAD), start, 2
        )
        grad_values = lax.dynamic_update_slice_in_dim(
            grad_values, part_values.reshape(groups, length, 2 * HEAD), start, 2
        )
        return (grad_query, grad_keys, grad_values)

    start_state = (
        jnp.zeros((groups, rows, width), jnp.float32),
        jnp.zeros((groups, length, width), jnp.float32),
        jnp.zeros((groups, length, width), jnp.float32),
    )
    return lax.fori_loop(0, width // (2 * HEAD), step, start_state)


def on_device(
    layer_input,
    doc_ids,
    attn_gain,
    query_weight,
    key_weight,
    value_weight,
    out_weight,
    mlp_gain,
    gate_weight,
    up_weight,
    down_weight,
    out_grad,
):
    groups, rows, width = layer_input.shape
    length = doc_ids.shape[1]
    gathered = (
        lax.all_gather(attn_gain, ("dp", "ctx"), axis=0, tiled=True),
        lax.all_gather(query_weight, ("dp", "ctx"), axis=0, tiled=True),
        lax.all_gather(key_weight, ("dp", "ctx"), axis=0, tiled=True),
        lax.all_gather(value_weight, ("dp", "ctx"), axis=0, tiled=True),
        lax.all_gather(out_weight, ("dp", "ctx"), axis=0, tiled=True),
        lax.all_gather(mlp_gain, ("dp", "ctx"), axis=0, tiled=True),
        lax.all_gather(gate_weight, ("dp", "ctx"), axis=0, tiled=True),
        lax.all_gather(up_weight, ("dp", "ctx"), axis=0, tiled=True),
        lax.all_gather(down_weight, ("dp", "ctx"), axis=0, tiled=True),
    )
    gain_one, w_query, w_key, w_value, w_out, gain_two, w_gate, w_up, w_down = gathered
    first = lax.axis_index("ctx") * rows
    places = jnp.arange(length)
    own_ids = lax.dynamic_slice_in_dim(doc_ids, first, rows, 1)
    own_places = first + jnp.arange(rows)
    allowed = (own_ids[:, :, None] == doc_ids[:, None, :]) & (
        places[None, None, :] <= own_places[None, :, None]
    )
    inputs = layer_input.reshape(groups * rows, width).astype(jnp.float32)
    gain_attn = gain_one.astype(jnp.float32)
    normed_full, inverse_one = normalize(inputs, gain_attn)
    normed = normed_full.astype(jnp.bfloat16)
    query = product(normed, w_query).astype(jnp.bfloat16).reshape(groups, rows, width)
    keys_own = product(normed, w_key).astype(jnp.bfloat16).reshape(groups, rows, width)
    values_own = product(normed, w_value).astype(jnp.bfloat16).reshape(groups, rows, width)
    keys, values = (
        lax.all_gather(keys_own, "ctx", axis=1, tiled=True),
        lax.all_gather(values_own, "ctx", axis=1, tiled=True),
    )
    attended, logsum = attend(query, keys, values, allowed)
    attended_rows = attended.reshape(groups * rows, width)
    middle = inputs + product(attended_rows, w_out)
    gain_mlp = gain_two.astype(jnp.float32)
    normed_two_full, inverse_two = normalize(middle, gain_mlp)
    normed_two = normed_two_full.astype(jnp.bfloat16)
    gate = product(normed_two, w_gate)
    upward = product(normed_two, w_up)
    sigma = jax.nn.sigmoid(gate)
    hidden = (gate * sigma * upward).astype(jnp.bfloat16)
    layer_output = (middle + product(hidden, w_down)).astype(jnp.bfloat16)
    gathered_back = (
        lax.all_gather(attn_gain, ("dp", "ctx"), axis=0, tiled=True),
        lax.all_gather(query_weight, ("dp", "ctx"), axis=0, tiled=True),
        lax.all_gather(key_weight, ("dp", "ctx"), axis=0, tiled=True),
        lax.all_gather(value_weight, ("dp", "ctx"), axis=0, tiled=True),
        lax.all_gather(out_weight, ("dp", "ctx"), axis=0, tiled=True),
        lax.all_gather(mlp_gain, ("dp", "ctx"), axis=0, tiled=True),
        lax.all_gather(gate_weight, ("dp", "ctx"), axis=0, tiled=True),
        lax.all_gather(up_weight, ("dp", "ctx"), axis=0, tiled=True),
        lax.all_gather(down_weight, ("dp", "ctx"), axis=0, tiled=True),
    )
    gain_one, w_query, w_key, w_value, w_out, gain_two, w_gate, w_up, w_down = gathered_back
    upstream = out_grad.reshape(groups * rows, width)
    down_grad = product_left(hidden, upstream)
    grad_hidden = product_right(upstream, w_down)
    grad_gate = (grad_hidden * upward * sigma * (1.0 + gate * (1.0 - sigma))).astype(jnp.bfloat16)
    grad_up = (grad_hidden * gate * sigma).astype(jnp.bfloat16)
    gate_grad = product_left(normed_two, grad_gate)
    up_grad = product_left(normed_two, grad_up)
    grad_normed_two = product_right(grad_gate, w_gate) + product_right(grad_up, w_up)
    grad_middle, mlp_gain_grad = norm_back(
        middle, inverse_two, gain_two.astype(jnp.float32), grad_normed_two
    )
    grad_middle = grad_middle + upstream.astype(jnp.float32)
    grad_branch = grad_middle.astype(jnp.bfloat16)
    out_proj_grad = product_left(attended_rows, grad_branch)
    grad_attended = (
        product_right(grad_branch, w_out).astype(jnp.bfloat16).reshape(groups, rows, width)
    )
    grad_query, grad_keys_all, grad_values_all = attend_back(
        query, keys, values, allowed, logsum, grad_attended
    )
    grad_keys, grad_values = (
        lax.psum_scatter(
            grad_keys_all.astype(jnp.bfloat16), "ctx", scatter_dimension=1, tiled=True
        ).astype(jnp.float32),
        lax.psum_scatter(
            grad_values_all.astype(jnp.bfloat16), "ctx", scatter_dimension=1, tiled=True
        ).astype(jnp.float32),
    )
    grad_query = grad_query.astype(jnp.bfloat16).reshape(groups * rows, width)
    grad_keys = grad_keys.astype(jnp.bfloat16).reshape(groups * rows, width)
    grad_values = grad_values.astype(jnp.bfloat16).reshape(groups * rows, width)
    query_grad = product_left(normed, grad_query)
    key_grad = product_left(normed, grad_keys)
    value_grad = product_left(normed, grad_values)
    grad_normed = (
        product_right(grad_query, w_query)
        + product_right(grad_keys, w_key)
        + product_right(grad_values, w_value)
    )
    grad_inputs, attn_gain_grad = norm_back(
        inputs, inverse_one, gain_one.astype(jnp.float32), grad_normed
    )
    input_grad = (grad_middle + grad_inputs).reshape(groups, rows, width)
    shares = (
        lax.psum_scatter(attn_gain_grad, ("dp", "ctx"), scatter_dimension=0, tiled=True),
        lax.psum_scatter(query_grad, ("dp", "ctx"), scatter_dimension=0, tiled=True),
        lax.psum_scatter(key_grad, ("dp", "ctx"), scatter_dimension=0, tiled=True),
        lax.psum_scatter(value_grad, ("dp", "ctx"), scatter_dimension=0, tiled=True),
        lax.psum_scatter(out_proj_grad, ("dp", "ctx"), scatter_dimension=0, tiled=True),
        lax.psum_scatter(mlp_gain_grad, ("dp", "ctx"), scatter_dimension=0, tiled=True),
        lax.psum_scatter(gate_grad, ("dp", "ctx"), scatter_dimension=0, tiled=True),
        lax.psum_scatter(up_grad, ("dp", "ctx"), scatter_dimension=0, tiled=True),
        lax.psum_scatter(down_grad, ("dp", "ctx"), scatter_dimension=0, tiled=True),
    )
    return (
        layer_output.reshape(groups, rows, width),
        input_grad,
        shares[0],
        shares[1],
        shares[2],
        shares[3],
        shares[4],
        shares[5],
        shares[6],
        shares[7],
        shares[8],
    )


def solution(mesh):
    placed = (
        P("dp", "ctx", None),
        P("dp", None),
        P(("dp", "ctx")),
        P(("dp", "ctx"), None),
        P(("dp", "ctx"), None),
        P(("dp", "ctx"), None),
        P(("dp", "ctx"), None),
        P(("dp", "ctx")),
        P(("dp", "ctx"), None),
        P(("dp", "ctx"), None),
        P(("dp", "ctx"), None),
        P("dp", "ctx", None),
    )
    return jax.shard_map(
        on_device,
        mesh=mesh,
        in_specs=placed,
        out_specs=(
            P("dp", "ctx", None),
            P("dp", "ctx", None),
            P(("dp", "ctx")),
            P(("dp", "ctx"), None),
            P(("dp", "ctx"), None),
            P(("dp", "ctx"), None),
            P(("dp", "ctx"), None),
            P(("dp", "ctx")),
            P(("dp", "ctx"), None),
            P(("dp", "ctx"), None),
            P(("dp", "ctx"), None),
        ),
        check_vma=False,
    )
```

profile of v0, /device:TPU:0, one launch (start us, length us, event | category | flops | bytes accessed | tf_op | source)
XLA Modules:
  0.0 2608.5 jit_solution(7120969927249212955)
XLA Ops:
  11.1 42.1 %all-reduce.5 = (bf16[1024]{0:T(1024)(128)(2,1)S(1)}, bf16[1024]{0:T(1024)(128)(2,1)S(1)}) all-reduce(bf16[1024]{0:T(1024)(128)(2,1)S(1)} %dynamic-update-slice, bf16[1024]{0:T(1024)(128)(2,1)S(1)} %dynamic-update-slice.1), channel_id=1, replica_groups=mesh['dp'=4,'ctx'=8] {'dp','ctx'}, use_global_device_ids=true, to_apply=%add | all-reduce | flops 2048 | bytes 8192
  55.8 14.4 all-gather.10.cloned.1.call-done
  70.3 2.3 convolution_convert_fusion.4
  73.7 55.0 %all-gather.16.cloned.1.call-done = bf16[1024,1024]{1,0:T(8,128)(2,1)} async-done(((bf16[32,1024]{1,0:T(8,128)(2,1)}), bf16[1024,1024]{1,0:T(8,128)(2,1)}) %all-gather.16.cloned.1.call-update) | async-done | bytes 2097168 | tf_op jit(solution)/shard_map/all_gather | solution.py:165
  128.7 2.3 convolution_convert_fusion.2
  135.4 51.7 %all-gather.14.cloned.1.call-done = bf16[1024,1024]{1,0:T(8,128)(2,1)} async-done(((bf16[32,1024]{1,0:T(8,128)(2,1)}), bf16[1024,1024]{1,0:T(8,128)(2,1)}) %all-gather.14.cloned.1.call-update) | async-done | bytes 2097168 | tf_op jit(solution)/shard_map/all_gather | solution.py:164
  187.1 2.3 convolution_convert_fusion.3
  190.4 73.1 %all-gather.12.cloned.1.call-done = bf16[2,1024,1024]{1,2,0:T(8,128)(2,1)} async-done(((bf16[2,128,1024]{1,2,0:T(8,128)(2,1)}), bf16[2,1024,1024]{1,2,0:T(8,128)(2,1)}) %all-gather.12.cloned.1.call-update) | async-done | bytes 4194320 | tf_op jit(solution)/shard_map/all_gather | solution.py:190
  263.4 75.7 %all-gather.18.cloned.1.call-done = bf16[2,1024,1024]{1,2,0:T(8,128)(2,1)} async-done(((bf16[2,128,1024]{1,2,0:T(8,128)(2,1)}), bf16[2,1024,1024]{1,2,0:T(8,128)(2,1)}) %all-gather.18.cloned.1.call-update) | async-done | bytes 4194320 | tf_op jit(solution)/shard_map/all_gather | solution.py:189
  340.0 56.5 %while.38 = (s32[]{:T(128)}, bf16[2,128,1024]{2,1,0:T(8,128)(2,1)}, f32[2,16,128]{2,1,0:T(8,128)S(1)}, bf16[2,1024,1024]{1,2,0:T(8,128)(2,1)}, bf16[2,128,1024]{...) while((s32[]{:T(128)}, bf16[2,128,1024]{2,1,0:T(8,128)(2,1)}, ...), condition=%wide.region_4.5_spmd.clone, body=%wide.region_1.4_spmd.clone.sunk | while | flops 141065728 | bytes 11166969 | solution.py:79
  340.0 2.2 constant_dynamic-slice_fusion.16
  347.1 2.1 constant_dynamic-slice_fusion.16
  354.2 2.1 constant_dynamic-slice_fusion.16
  368.3 2.1 constant_dynamic-slice_fusion.16
  375.3 2.1 constant_dynamic-slice_fusion.16
  382.4 2.1 constant_dynamic-slice_fusion.16
  389.4 2.1 constant_dynamic-slice_fusion.16
  396.9 2.6 multiply_reduce_fusion.5
  399.7 76.4 %all-gather.22.cloned.1.call-done = bf16[1024,4096]{1,0:T(8,128)(2,1)} async-done(((bf16[32,4096]{1,0:T(8,128)(2,1)}), bf16[1024,4096]{1,0:T(8,128)(2,1)}) %all-gather.22.cloned.1.call-update) | async-done | bytes 8388624 | tf_op jit(solution)/shard_map/all_gather | solution.py:169
  476.1 7.7 fusion.17
  483.8 71.3 %all-gather.24.cloned.1.call-done = bf16[1024,4096]{1,0:T(8,128)(2,1)} async-done(((bf16[32,4096]{1,0:T(8,128)(2,1)}), bf16[1024,4096]{1,0:T(8,128)(2,1)}) %all-gather.24.cloned.1.call-update) | async-done | bytes 8388624 | tf_op jit(solution)/shard_map/all_gather | solution.py:170
  555.1 7.7 fusion.18
  562.8 71.3 %all-gather.26.cloned.1.call-done = bf16[4096,1024]{1,0:T(8,128)(2,1)} async-done(((bf16[128,1024]{1,0:T(8,128)(2,1)}), bf16[4096,1024]{1,0:T(8,128)(2,1)}) %all-gather.26.cloned.1.call-update) | async-done | bytes 8388624 | tf_op jit(solution)/shard_map/all_gather | solution.py:171
  634.1 12.9 multiply_convert_fusion.1
  647.0 7.3 fusion.19
  654.3 2.6 multiply_reduce_fusion.1
  660.5 2.5 broadcast.154.clone
  663.0 2.6 broadcast.154.clone2
  666.4 99.2 %while.39 = (s32[]{:T(128)}, bf16[2,128,1024]{2,1,0:T(8,128)(2,1)}, bf16[2,1024,1024]{2,1,0:T(8,128)(2,1)}, bf16[2,1024,1024]{2,1,0:T(8,128)(2,1)}, bf16[2,1024,...) while((s32[]{:T(128)}, bf16[2,128,1024]{2,1,0:T(8,128)(2,1)}, ...), condition=%wide.region_9.0_spmd.clone, body=%wide.region_7.0_spmd.clone.sunk | while | flops 341376512 | bytes 38882672 | solution.py:143
  766.8 2.8 convolution_bitcast_fusion.2
  771.0 2.7 fusion.12
  773.9 78.4 %reduce-scatter.10.cloned.1.call-done = bf16[2,128,1024]{2,1,0:T(8,128)(2,1)} async-done(((bf16[2,1024,1024]{2,1,0:T(8,128)(2,1)}), bf16[2,128,1024]{2,1,0:T(8,128)(2,1)}) %reduce-scatter.10.cloned.1.call-update) | async-done | bytes 524304 | tf_op jit(solution)/shard_map/reduce_scatter | solution.py:236
  852.4 3.8 convolution_bitcast_fusion.1
  856.3 88.0 %reduce-scatter.12.cloned.1.call-done = bf16[2,128,1024]{2,1,0:T(8,128)(2,1)} async-done(((bf16[2,1024,1024]{2,1,0:T(8,128)(2,1)}), bf16[2,128,1024]{2,1,0:T(8,128)(2,1)}) %reduce-scatter.12.cloned.1.call-update) | async-done | bytes 524304 | tf_op jit(solution)/shard_map/reduce_scatter | solution.py:239
  944.3 3.9 convolution_bitcast_fusion
  949.2 9.7 fusion.21
  959.0 9.7 fusion.22
  969.8 9.7 fusion.23
  979.5 2.5 fusion.20
  982.1 6.7 fusion.11
  991.7 42.6 %all-reduce.4 = (f32[1024]{0:T(1024)S(1)}, f32[1024]{0:T(1024)S(1)}) all-reduce(f32[1024]{0:T(1024)S(1)} %get-tuple-element.554, f32[1024]{0:T(1024)S(1)} %get-tuple-element.552), channel_id=4, replica_groups=mesh['dp'=4,'ctx'=8] {'dp','ctx'}, use_global_device_ids=true, to_apply=%region_14.15.clone | all-reduce | flops 2048 | bytes 16384
  1036.6 54.6 %reduce-scatter.14.cloned.1.call-done = f32[32,1024]{1,0:T(8,128)} async-done(((f32[1024,1024]{1,0:T(8,128)}), f32[32,1024]{1,0:T(8,128)}) %reduce-scatter.14.cloned.1.call-update) | async-done | bytes 131088 | tf_op jit(solution)/shard_map/reduce_scatter | solution.py:260
  1091.3 143.7 %reduce-scatter.20.cloned.1.call-done = f32[32,1024]{1,0:T(8,128)} async-done(((f32[1024,1024]{1,0:T(8,128)}), f32[32,1024]{1,0:T(8,128)}) %reduce-scatter.20.cloned.1.call-update) | async-done | bytes 131088 | tf_op jit(solution)/shard_map/reduce_scatter | solution.py:263
  1234.9 143.8 %reduce-scatter.16.cloned.1.call-done = f32[32,1024]{1,0:T(8,128)} async-done(((f32[1024,1024]{1,0:T(8,128)}), f32[32,1024]{1,0:T(8,128)}) %reduce-scatter.16.cloned.1.call-update) | async-done | bytes 131088 | tf_op jit(solution)/shard_map/reduce_scatter | solution.py:261
  1378.7 143.8 %reduce-scatter.18.cloned.1.call-done = f32[32,1024]{1,0:T(8,128)} async-done(((f32[1024,1024]{1,0:T(8,128)}), f32[32,1024]{1,0:T(8,128)}) %reduce-scatter.18.cloned.1.call-update) | async-done | bytes 131088 | tf_op jit(solution)/shard_map/reduce_scatter | solution.py:262
  1522.6 358.7 %reduce-scatter.22.cloned.1.call-done = f32[32,4096]{1,0:T(8,128)} async-done(((f32[1024,4096]{1,0:T(8,128)}), f32[32,4096]{1,0:T(8,128)}) %reduce-scatter.22.cloned.1.call-update) | async-done | bytes 524304 | tf_op jit(solution)/shard_map/reduce_scatter | solution.py:265
  1881.3 360.0 %reduce-scatter.24.cloned.1.call-done = f32[32,4096]{1,0:T(8,128)} async-done(((f32[1024,4096]{1,0:T(8,128)}), f32[32,4096]{1,0:T(8,128)}) %reduce-scatter.24.cloned.1.call-update) | async-done | bytes 524304 | tf_op jit(solution)/shard_map/reduce_scatter | solution.py:266
  2241.3 360.1 %reduce-scatter.26.cloned.1.call-done = f32[128,1024]{1,0:T(8,128)} async-done(((f32[4096,1024]{1,0:T(8,128)}), f32[128,1024]{1,0:T(8,128)}) %reduce-scatter.26.cloned.1.call-update) | async-done | bytes 524304 | tf_op jit(solution)/shard_map/reduce_scatter | solution.py:267
  (371 shorter events, 168.6 us)
Async XLA Ops:
  7.2 63.1 %all-gather.10.cloned.1.call-start = ((), (), s32[]{:S(2)}) async-start(), calls=%async_computation.9 | async-start | bytes 2162688 | tf_op jit(solution)/shard_map/all_gather | solution.py:166
  7.9 120.8 %all-gather.16.cloned.1.call-start = ((), (), s32[]{:S(2)}) async-start(), calls=%async_computation.12 | async-start | bytes 2162688 | tf_op jit(solution)/shard_map/all_gather | solution.py:165
  8.7 178.4 %all-gather.14.cloned.1.call-start = ((), (), s32[]{:S(2)}) async-start(), calls=%async_computation.11 | async-start | bytes 2162688 | tf_op jit(solution)/shard_map/all_gather | solution.py:164
  9.4 254.1 %all-gather.12.cloned.1.call-start = ((), (), s32[]{:S(2)}) async-start(), calls=%async_computation.10 | async-start | bytes 4718592 | tf_op jit(solution)/shard_map/all_gather | solution.py:190
  54.5 18.2 copy-start.24
  73.6 265.5 %all-gather.18.cloned.1.call-start = ((), (), s32[]{:S(2)}) async-start(), calls=%async_computation.13 | async-start | bytes 4718592 | tf_op jit(solution)/shard_map/all_gather | solution.py:189
  131.0 4.4 copy-start.23
  132.0 264.8 %all-gather.20.cloned.1.call-start = ((), (), s32[]{:S(2)}) async-start(), calls=%async_computation.14 | async-start | bytes 2162688 | tf_op jit(solution)/shard_map/all_gather | solution.py:167
  132.6 343.4 %all-gather.22.cloned.1.call-start = ((), (), s32[]{:S(2)}) async-start(), calls=%async_computation.15 | async-start | bytes 8650752 | tf_op jit(solution)/shard_map/all_gather | solution.py:169
  133.4 421.7 %all-gather.24.cloned.1.call-start = ((), (), s32[]{:S(2)}) async-start(), calls=%async_computation.16 | async-start | bytes 8650752 | tf_op jit(solution)/shard_map/all_gather | solution.py:170
  134.1 500.0 %all-gather.26.cloned.1.call-start = ((), (), s32[]{:S(2)}) async-start(), calls=%async_computation.17 | async-start | bytes 8650752 | tf_op jit(solution)/shard_map/all_gather | solution.py:171
  134.9 717.5 %reduce-scatter.10.cloned.1.call-start = ((), (), s32[]{:S(2)}) async-start(), calls=%async_computation.18 | async-start | bytes 4718592 | tf_op jit(solution)/shard_map/reduce_scatter | solution.py:236
  340.0 56.9 %copy-start.3 = (bf16[2,128,1024]{2,1,0:T(8,128)(2,1)S(1)}, bf16[2,128,1024]{2,1,0:T(8,128)(2,1)}, u32[]{:S(2)}) copy-start(bf16[2,128,1024]{2,1,0:T(8,128)(2,1)} %param.16) | copy-start | bytes 1572868
  399.5 257.5 %copy-start.7 = (f32[256,1024]{1,0:T(8,128)}, f32[256,1024]{1,0:T(8,128)S(1)}, u32[]{:S(2)}) copy-start(f32[256,1024]{1,0:T(8,128)S(1)} %get-tuple-element.616) | copy-start | bytes 3145732
  399.6 155.4 %copy-start.10 = (bf16[256,1024]{1,0:T(8,128)(2,1)}, bf16[256,1024]{1,0:T(8,128)(2,1)S(1)}, u32[]{:S(2)}) copy-start(bf16[256,1024]{1,0:T(8,128)(2,1)S(1)} %multiply_convert_fusion.5) | copy-start | bytes 1572868
  483.8 150.3 %copy-start.19 = (bf16[2,128,1024]{2,1,0:T(8,128)(2,1)S(1)}, bf16[2,128,1024]{2,1,0:T(8,128)(2,1)}, u32[]{:S(2)}) copy-start(bf16[2,128,1024]{2,1,0:T(8,128)(2,1)} %param.27) | copy-start | bytes 1572868
  647.0 7.3 copy-start.22
  647.0 7.3 copy-start.21
  647.0 7.3 copy-start.26
  657.0 2.0 copy-start.9
  670.0 2.2 copy-start.1
  676.1 1.4 copy-start.2
  682.4 2.2 copy-start.1
  688.5 1.5 copy-start.2
  694.8 2.2 copy-start.1
  700.9 1.5 copy-start.2
  707.3 2.2 copy-start.1
  719.7 2.2 copy-start.1
  732.0 2.2 copy-start.1
  738.1 1.4 copy-start.2
  744.4 2.2 copy-start.1
  750.5 1.4 copy-start.2
  756.8 2.2 copy-start.1
  762.9 1.4 copy-start.2
  765.6 178.7 %reduce-scatter.12.cloned.1.call-start = ((), (), s32[]{:S(2)}) async-start(), calls=%async_computation.19 | async-start | bytes 4718592 | tf_op jit(solution)/shard_map/reduce_scatter | solution.py:239
  766.3 325.0 %reduce-scatter.14.cloned.1.call-start = ((), (), s32[]{:S(2)}) async-start(), calls=%async_computation.20 | async-start | bytes 4325376 | tf_op jit(solution)/shard_map/reduce_scatter | solution.py:260
  769.6 465.3 %reduce-scatter.20.cloned.1.call-start = ((), (), s32[]{:S(2)}) async-start(), calls=%async_computation.23 | async-start | bytes 4325376 | tf_op jit(solution)/shard_map/reduce_scatter | solution.py:263
  773.7 605.0 %reduce-scatter.16.cloned.1.call-start = ((), (), s32[]{:S(2)}) async-start(), calls=%async_computation.21 | async-start | bytes 4325376 | tf_op jit(solution)/shard_map/reduce_scatter | solution.py:261
  856.3 666.3 %reduce-scatter.18.cloned.1.call-start = ((), (), s32[]{:S(2)}) async-start(), calls=%async_computation.22 | async-start | bytes 4325376 | tf_op jit(solution)/shard_map/reduce_scatter | solution.py:262
  948.2 933.1 %reduce-scatter.22.cloned.1.call-start = ((), (), s32[]{:S(2)}) async-start(), calls=%async_computation.24 | async-start | bytes 17301504 | tf_op jit(solution)/shard_map/reduce_scatter | solution.py:265
  959.0 1282.4 %reduce-scatter.24.cloned.1.call-start = ((), (), s32[]{:S(2)}) async-start(), calls=%async_computation.25 | async-start | bytes 17301504 | tf_op jit(solution)/shard_map/reduce_scatter | solution.py:266
  968.8 1632.7 %reduce-scatter.26.cloned.1.call-start = ((), (), s32[]{:S(2)}) async-start(), calls=%async_computation.26 | async-start | bytes 17301504 | tf_op jit(solution)/shard_map/reduce_scatter | solution.py:267
  979.5 2.5 copy-start.8
  979.5 2.6 copy-start.14
  982.1 6.7 copy-start.15
  982.1 6.7 copy-start.18
  988.8 1.8 copy-start.17
  988.8 1.8 copy-start.25
  (18 other events, 22.6 us)
Sparse Core Ops, SparseCore 0:
  11.0 59.2 all-gather.9
  73.3 55.3 all-gather.15
  131.7 55.3 all-gather.13
  189.5 73.8 all-gather.11
  265.9 73.1 all-gather.17
  342.0 54.8 all-gather.19
  399.9 76.1 all-gather.21
  479.0 75.9 all-gather.23
  558.1 75.9 all-gather.25
  765.7 86.6 reduce-scatter.9
  856.4 87.8 reduce-scatter.11
  947.0 144.2 reduce-scatter.13
  1094.1 140.7 reduce-scatter.19
  1237.6 141.0 reduce-scatter.15
  1381.4 141.1 reduce-scatter.17
  1525.3 355.9 reduce-scatter.21
  1884.0 357.2 reduce-scatter.23
  2244.0 357.3 reduce-scatter.25
where the time goes:
time: 2620 us; the launch traced here: 2610 us
  waiting for transfers between devices  2230 us (85%)
  matrix products  155 us (6%)
  local copies, waits for them, and re-layouts  108 us (4%)
  blocking collectives  84.6 us (3%)
    reduce_scatter x1, waiting for transfers between devices, on_device(): lax.psum_scatter(down_grad, ('dp', 'ctx'), scatter_dimension=0, tiled=True)  360 us
    reduce_scatter x1, waiting for transfers between devices, on_device(): lax.psum_scatter(up_grad, ('dp', 'ctx'), scatter_dimension=0, tiled=True)  360 us
    reduce_scatter x1, waiting for transfers between devices, on_device(): lax.psum_scatter(gate_grad, ('dp', 'ctx'), scatter_dimension=0, tiled=True)  359 us
    reduce_scatter x1, waiting for transfers between devices, on_device(): lax.psum_scatter(value_grad, ('dp', 'ctx'), scatter_dimension=0, tiled=True)  144 us
    reduce_scatter x1, waiting for transfers between devices, on_device(): lax.psum_scatter(key_grad, ('dp', 'ctx'), scatter_dimension=0, tiled=True)  144 us
    reduce_scatter x1, waiting for transfers between devices, on_device(): lax.psum_scatter(out_proj_grad, ('dp', 'ctx'), scatter_dimension=0, tiled...  144 us
    reduce_scatter x1, waiting for transfers between devices, on_device(): lax.psum_scatter(grad_values_all.astype(jnp.bfloat16), 'ctx', scatter_dim...  88 us
    unnamed x2, blocking collectives  84.6 us
  transfers between devices with their start and end apart: 18, of which 18 were waited for; matrix products, arithmetic and copies ran while one was open for 6% of the time, Pallas kernels for 0%

commit v1 on v0

--- a/solution.py
+++ b/solution.py
@@ -5,6 +5,28 @@
 
 HEAD = 64
 EPS = 1e-05
+
+
+def laid_out(blocks, dim):
+    blocks = jnp.moveaxis(blocks, 0, dim)
+    shape = blocks.shape
+    return blocks.reshape(*shape[:dim], shape[dim] * shape[dim + 1], *shape[dim + 2 :])
+
+
+def collect(x, axis, dim):
+    size = lax.axis_size(axis)
+    pairs = [(i, (i + 1) % size) for i in range(size)]
+    back = [(b, a) for a, b in pairs]
+    lower, upper = ([], [])
+    for lap in range(size - 1):
+        if lap % 2 == 0:
+            lower.append(lax.ppermute(lower[-1] if lower else x, axis, pairs))
+        else:
+            upper.append(lax.ppermute(upper[-1] if upper else x, axis, back))
+    tiles = jnp.stack([*lower[::-1], x, *upper])
+    shift = lax.axis_index(axis) - len(lower)
+    tiles = tiles[(jnp.arange(size) - shift) % size]
+    return laid_out(tiles, dim)
 
 
 def product(left, right):
@@ -187,7 +209,7 @@
     values_own = product(normed, w_value).astype(jnp.bfloat16).reshape(groups, rows, width)
     keys, values = (
         lax.all_gather(keys_own, "ctx", axis=1, tiled=True),
-        lax.all_gather(values_own, "ctx", axis=1, tiled=True),
+        collect(values_own, "ctx", 1),
     )
     attended, logsum = attend(query, keys, values, allowed)
     attended_rows = attended.reshape(groups * rows, width)

time: 2620 us -> 2570 us (0.981)
  waiting for transfers between devices: 2230 us -> 2140 us
  starting transfers between devices: 1.4 us -> 28.7 us
    all_gather x1 -> x0, waiting for transfers between devices: 73.1 us -> none  [on_device(): lax.all_gather(values_own, 'ctx', axis=1, tiled=True)]
    ppermute x0 -> x7, waiting for transfers between devices: none -> 60.7 us  [the longest x4 52 us: collect(): lower.append(lax.ppermute(lower[-1] if lower else x, axis, pairs))]
    all_gather x1, waiting for transfers between devices: 51.7 us -> 0.02 us  [on_device(): lax.all_gather(query_weight, ('dp', 'ctx'), axis=0, tiled=True)]
    all_gather x1, waiting for transfers between devices: 55 us -> 14 us  [on_device(): lax.all_gather(key_weight, ('dp', 'ctx'), axis=0, tiled=True)]
    all_gather x1, waiting for transfers between devices: 14.4 us -> 53.1 us  [on_device(): lax.all_gather(value_weight, ('dp', 'ctx'), axis=0, tiled=True)]
    all_gather x1, waiting for transfers between devices: 75.7 us -> 37.9 us  [on_device(): lax.all_gather(keys_own, 'ctx', axis=1, tiled=True)]
    ppermute x0 -> x7, starting transfers between devices: none -> 27.7 us  [the longest x3 21.2 us: collect(): upper.append(lax.ppermute(upper[-1] if upper else x, axis, back))]
  transfers between devices with their start and end apart: 18 -> 24, of which waited for: 18 -> 21; matrix products, arithmetic and copies ran while one was open for 6% -> 6% of each run, Pallas kernels for 0% -> 0%
where the time goes in v1:
time: 2570 us; the launch traced here: 2560 us
  waiting for transfers between devices  2140 us (83%)
  matrix products  149 us (6%)
  local copies, waits for them, and re-layouts  122 us (5%)
  blocking collectives  84.3 us (3%)
  starting transfers between devices  28.7 us (1%)
    reduce_scatter x1, waiting for transfers between devices, on_device(): lax.psum_scatter(down_grad, ('dp', 'ctx'), scatter_dimension=0, tiled=True)  360 us
    reduce_scatter x1, waiting for transfers between devices, on_device(): lax.psum_scatter(up_grad, ('dp', 'ctx'), scatter_dimension=0, tiled=True)  360 us
    reduce_scatter x1, waiting for transfers between devices, on_device(): lax.psum_scatter(gate_grad, ('dp', 'ctx'), scatter_dimension=0, tiled=True)  359 us
    reduce_scatter x1, waiting for transfers between devices, on_device(): lax.psum_scatter(key_grad, ('dp', 'ctx'), scatter_dimension=0, tiled=True)  144 us
    reduce_scatter x1, waiting for transfers between devices, on_device(): lax.psum_scatter(value_grad, ('dp', 'ctx'), scatter_dimension=0, tiled=True)  144 us
    reduce_scatter x1, waiting for transfers between devices, on_device(): lax.psum_scatter(out_proj_grad, ('dp', 'ctx'), scatter_dimension=0, tiled...  143 us
    reduce_scatter x1, waiting for transfers between devices, on_device(): lax.psum_scatter(grad_values_all.astype(jnp.bfloat16), 'ctx', scatter_dim...  87.7 us
    unnamed x2, blocking collectives  84.3 us
  transfers between devices with their start and end apart: 24, of which 21 were waited for; matrix products, arithmetic and copies ran while one was open for 6% of the time, Pallas kernels for 0%

profile of v1, /device:TPU:0, one launch (start us, length us, event | category | flops | bytes accessed | tf_op | source)
XLA Modules:
  0.0 2558.3 jit_solution(722697486270216222)
XLA Ops:
  11.1 42.1 %all-reduce.5 = (bf16[1024]{0:T(1024)(128)(2,1)S(1)}, bf16[1024]{0:T(1024)(128)(2,1)S(1)}) all-reduce(bf16[1024]{0:T(1024)(128)(2,1)S(1)} %dynamic-update-slice, bf16[1024]{0:T(1024)(128)(2,1)S(1)} %dynamic-update-slice.1), channel_id=1, replica_groups=mesh['dp'=4,'ctx'=8] {'dp','ctx'}, use_global_device_ids=true, to_apply=%add | all-reduce | flops 2048 | bytes 8192
  56.3 14.0 all-gather.13.cloned.1.call-done
  75.6 53.1 %all-gather.9.cloned.1.call-done = bf16[1024,1024]{1,0:T(8,128)(2,1)} async-done(((bf16[32,1024]{1,0:T(8,128)(2,1)}), bf16[1024,1024]{1,0:T(8,128)(2,1)}) %all-gather.9.cloned.1.call-update) | async-done | bytes 2097168 | tf_op jit(solution)/shard_map/all_gather | solution.py:188
  132.5 16.1 collective-permute-done
  148.6 4.7 collective-permute-start.4
  153.3 19.2 collective-permute-done.1
  172.5 2.5 collective-permute-start.2
  175.2 11.6 collective-permute-start.5
  186.7 13.9 collective-permute-done.2
  203.3 3.1 convolution_convert_fusion.3
  208.4 4.9 collective-permute-start.6
  213.3 2.8 collective-permute-done.3
  224.1 8.8 collective-permute-done.6
  233.8 5.0 gather_fusion
  238.7 6.8 copy.46
  245.5 7.4 reshape.326
  252.9 37.9 %all-gather.15.cloned.1.call-done = bf16[2,1024,1024]{1,2,0:T(8,128)(2,1)} async-done(((bf16[2,128,1024]{1,2,0:T(8,128)(2,1)}), bf16[2,1024,1024]{1,2,0:T(8,128)(2,1)}) %all-gather.15.cloned.1.call-update) | async-done | bytes 4194320 | tf_op jit(solution)/shard_map/all_gather | solution.py:211
  290.9 37.4 %while.38 = (s32[]{:T(128)}, bf16[2,128,1024]{2,1,0:T(8,128)(2,1)S(1)}, f32[2,16,128]{2,1,0:T(8,128)S(1)}, bf16[2,1024,1024]{1,2,0:T(8,128)(2,1)}, bf16[2,128,10...) while((s32[]{:T(128)}, ...), condition=%wide.region_4.5_spmd.clone, body=%wide.region_1.4_spmd.clone.sunk | while | flops 141065728 | bytes 11166977 | solution.py:101
  328.4 20.0 all-gather.17.cloned.1.call-done
  351.0 76.5 %all-gather.19.cloned.1.call-done = bf16[1024,4096]{1,0:T(8,128)(2,1)} async-done(((bf16[32,4096]{1,0:T(8,128)(2,1)}), bf16[1024,4096]{1,0:T(8,128)(2,1)}) %all-gather.19.cloned.1.call-update) | async-done | bytes 8388624 | tf_op jit(solution)/shard_map/all_gather | solution.py:191
  427.5 7.7 fusion.19
  435.2 71.3 %all-gather.21.cloned.1.call-done = bf16[1024,4096]{1,0:T(8,128)(2,1)} async-done(((bf16[32,4096]{1,0:T(8,128)(2,1)}), bf16[1024,4096]{1,0:T(8,128)(2,1)}) %all-gather.21.cloned.1.call-update) | async-done | bytes 8388624 | tf_op jit(solution)/shard_map/all_gather | solution.py:192
  506.5 7.7 fusion.20
  514.2 71.3 %all-gather.23.cloned.1.call-done = bf16[4096,1024]{1,0:T(8,128)(2,1)} async-done(((bf16[128,1024]{1,0:T(8,128)(2,1)}), bf16[4096,1024]{1,0:T(8,128)(2,1)}) %all-gather.23.cloned.1.call-update) | async-done | bytes 8388624 | tf_op jit(solution)/shard_map/all_gather | solution.py:193
  585.6 12.9 multiply_convert_fusion.1
  598.5 7.3 fusion.21
  605.8 2.7 multiply_reduce_fusion.1
  612.2 2.5 broadcast.218.clone
  614.7 2.6 broadcast.218.clone2
  617.3 99.7 %while.39 = (s32[]{:T(128)}, bf16[2,128,1024]{2,1,0:T(8,128)(2,1)}, bf16[2,1024,1024]{2,1,0:T(8,128)(2,1)}, bf16[2,1024,1024]{2,1,0:T(8,128)(2,1)}, bf16[2,1024,...) while((s32[]{:T(128)}, bf16[2,128,1024]{2,1,0:T(8,128)(2,1)}, ...), condition=%wide.region_9.10_spmd.clone, body=%wide.region_7.9_spmd.clone.sunk | while | flops 341376512 | bytes 38882680 | solution.py:165
  718.1 2.8 convolution_bitcast_fusion.2
  721.0 2.7 fusion.12
  724.0 79.7 %reduce-scatter.10.cloned.1.call-done = bf16[2,128,1024]{2,1,0:T(8,128)(2,1)} async-done(((bf16[2,1024,1024]{2,1,0:T(8,128)(2,1)}), bf16[2,128,1024]{2,1,0:T(8,128)(2,1)}) %reduce-scatter.10.cloned.1.call-update) | async-done | bytes 524304 | tf_op jit(solution)/shard_map/reduce_scatter | solution.py:258
  803.8 3.8 convolution_bitcast_fusion.1
  807.7 87.7 %reduce-scatter.12.cloned.1.call-done = bf16[2,128,1024]{2,1,0:T(8,128)(2,1)} async-done(((bf16[2,1024,1024]{2,1,0:T(8,128)(2,1)}), bf16[2,128,1024]{2,1,0:T(8,128)(2,1)}) %reduce-scatter.12.cloned.1.call-update) | async-done | bytes 524304 | tf_op jit(solution)/shard_map/reduce_scatter | solution.py:261
  895.4 3.9 convolution_bitcast_fusion
  899.3 9.7 fusion.23
  909.1 9.7 fusion.24
  919.9 9.7 fusion.25
  932.1 7.3 fusion.11
  942.2 42.2 %all-reduce.4 = (f32[1024]{0:T(1024)S(1)}, f32[1024]{0:T(1024)S(1)}) all-reduce(f32[1024]{0:T(1024)S(1)} %get-tuple-element.554, f32[1024]{0:T(1024)S(1)} %get-tuple-element.552), channel_id=4, replica_groups=mesh['dp'=4,'ctx'=8] {'dp','ctx'}, use_global_device_ids=true, to_apply=%region_14.15.clone | all-reduce | flops 2048 | bytes 16384
  986.8 55.1 %reduce-scatter.14.cloned.1.call-done = f32[32,1024]{1,0:T(8,128)} async-done(((f32[1024,1024]{1,0:T(8,128)}), f32[32,1024]{1,0:T(8,128)}) %reduce-scatter.14.cloned.1.call-update) | async-done | bytes 131088 | tf_op jit(solution)/shard_map/reduce_scatter | solution.py:282
  1041.9 142.9 %reduce-scatter.20.cloned.1.call-done = f32[32,1024]{1,0:T(8,128)} async-done(((f32[1024,1024]{1,0:T(8,128)}), f32[32,1024]{1,0:T(8,128)}) %reduce-scatter.20.cloned.1.call-update) | async-done | bytes 131088 | tf_op jit(solution)/shard_map/reduce_scatter | solution.py:285
  1184.8 143.9 %reduce-scatter.16.cloned.1.call-done = f32[32,1024]{1,0:T(8,128)} async-done(((f32[1024,1024]{1,0:T(8,128)}), f32[32,1024]{1,0:T(8,128)}) %reduce-scatter.16.cloned.1.call-update) | async-done | bytes 131088 | tf_op jit(solution)/shard_map/reduce_scatter | solution.py:283
  1328.8 143.8 %reduce-scatter.18.cloned.1.call-done = f32[32,1024]{1,0:T(8,128)} async-done(((f32[1024,1024]{1,0:T(8,128)}), f32[32,1024]{1,0:T(8,128)}) %reduce-scatter.18.cloned.1.call-update) | async-done | bytes 131088 | tf_op jit(solution)/shard_map/reduce_scatter | solution.py:284
  1472.6 358.9 %reduce-scatter.22.cloned.1.call-done = f32[32,4096]{1,0:T(8,128)} async-done(((f32[1024,4096]{1,0:T(8,128)}), f32[32,4096]{1,0:T(8,128)}) %reduce-scatter.22.cloned.1.call-update) | async-done | bytes 524304 | tf_op jit(solution)/shard_map/reduce_scatter | solution.py:287
  1831.4 360.1 %reduce-scatter.24.cloned.1.call-done = f32[32,4096]{1,0:T(8,128)} async-done(((f32[1024,4096]{1,0:T(8,128)}), f32[32,4096]{1,0:T(8,128)}) %reduce-scatter.24.cloned.1.call-update) | async-done | bytes 524304 | tf_op jit(solution)/shard_map/reduce_scatter | solution.py:288
  2191.5 360.1 %reduce-scatter.26.cloned.1.call-done = f32[128,1024]{1,0:T(8,128)} async-done(((f32[4096,1024]{1,0:T(8,128)}), f32[128,1024]{1,0:T(8,128)}) %reduce-scatter.26.cloned.1.call-update) | async-done | bytes 524304 | tf_op jit(solution)/shard_map/reduce_scatter | solution.py:289
  (394 shorter events, 181.9 us)
Async XLA Ops:
  7.2 63.1 %all-gather.13.cloned.1.call-start = ((), (), s32[]{:S(2)}) async-start(), calls=%async_computation.11 | async-start | bytes 2162688 | tf_op jit(solution)/shard_map/all_gather | solution.py:187
  7.9 120.8 %all-gather.9.cloned.1.call-start = ((), (), s32[]{:S(2)}) async-start(), calls=%async_computation.9 | async-start | bytes 2162688 | tf_op jit(solution)/shard_map/all_gather | solution.py:188
  8.7 194.6 %all-gather.11.cloned.1.call-start = ((), (), s32[]{:S(2)}) async-start(), calls=%async_computation.10 | async-start | bytes 2162688 | tf_op jit(solution)/shard_map/all_gather | solution.py:186
  9.4 281.4 %all-gather.15.cloned.1.call-start = ((), (), s32[]{:S(2)}) async-start(), calls=%async_computation.12 | async-start | bytes 4718592 | tf_op jit(solution)/shard_map/all_gather | solution.py:211
  56.3 118.8 %copy-start.23 = (s32[2,1024]{1,0:T(2,128)S(1)}, s32[2,1024]{1,0:T(2,128)}, u32[]{:S(2)}) copy-start(s32[2,1024]{1,0:T(2,128)} %param.17) | copy-start | bytes 24580
  73.6 274.8 %all-gather.17.cloned.1.call-start = ((), (), s32[]{:S(2)}) async-start(), calls=%async_computation.13 | async-start | bytes 2162688 | tf_op jit(solution)/shard_map/all_gather | solution.py:189
  74.2 353.3 %all-gather.19.cloned.1.call-start = ((), (), s32[]{:S(2)}) async-start(), calls=%async_computation.14 | async-start | bytes 8650752 | tf_op jit(solution)/shard_map/all_gather | solution.py:191
  74.8 431.7 %all-gather.21.cloned.1.call-start = ((), (), s32[]{:S(2)}) async-start(), calls=%async_computation.15 | async-start | bytes 8650752 | tf_op jit(solution)/shard_map/all_gather | solution.py:192
  75.5 510.0 %all-gather.23.cloned.1.call-start = ((), (), s32[]{:S(2)}) async-start(), calls=%async_computation.16 | async-start | bytes 8650752 | tf_op jit(solution)/shard_map/all_gather | solution.py:193
  131.0 17.6 collective-permute-start
  148.6 23.9 collective-permute-start.1
  148.6 26.5 %collective-permute-start.4 = (bf16[2,128,1024]{2,1,0:T(8,128)(2,1)S(1)}, bf16[2,128,1024]{2,1,0:T(8,128)(2,1)S(1)}, u32[]{:S(2)}, u32[]{:S(2)}) collective-permute-start(bf16[2,128,1024]{2,1,0:T(8,128)(2,1)S(1)} %bitcast.192), channel_id=1, source_target_pairs={{1,0},{2,1},{3,2},{4,3},{5,4},{6,5},{7,6},{0,7},{9,8},{10,9},{11,1... | collective-permute-start | bytes 1572872 | tf_op jit(solution)/shard_map/ppermute | solution.py:25
  172.5 28.1 %collective-permute-start.2 = (bf16[2,128,1024]{2,1,0:T(8,128)(2,1)S(1)}, bf16[2,128,1024]{2,1,0:T(8,128)(2,1)S(1)}, u32[]{:S(2)}, u32[]{:S(2)}) collective-permute-start(bf16[2,128,1024]{2,1,0:T(8,128)(2,1)S(1)} %collective-permute-done.1), channel_id=1, source_target_pairs={{0,1},{1,2},{2,3},{3,4},{4,5},{5,6},{6,7},{7,0},{8,9},{9,10},{10,1... | collective-permute-start | bytes 1572872 | tf_op jit(solution)/shard_map/ppermute | solution.py:23
  175.0 628.7 %reduce-scatter.10.cloned.1.call-start = ((), (), s32[]{:S(2)}) async-start(), calls=%async_computation.17 | async-start | bytes 4718592 | tf_op jit(solution)/shard_map/reduce_scatter | solution.py:258
  175.2 33.2 %collective-permute-start.5 = (bf16[2,128,1024]{2,1,0:T(8,128)(2,1)S(1)}, bf16[2,128,1024]{2,1,0:T(8,128)(2,1)}, u32[]{:S(2)}, u32[]{:S(2)}) collective-permute-start(bf16[2,128,1024]{2,1,0:T(8,128)(2,1)S(1)} %collective-permute-done.4), channel_id=1, source_target_pairs={{1,0},{2,1},{3,2},{4,3},{5,4},{6,5},{7,6},{0,7},{9,8},{10,9},{11,1... | collective-permute-start | bytes 1572872 | tf_op jit(solution)/shard_map/ppermute | solution.py:25
  200.6 15.6 collective-permute-start.3
  208.4 24.5 collective-permute-start.6
  290.9 57.5 %copy-start.3 = (bf16[2,128,1024]{2,1,0:T(8,128)(2,1)S(1)}, bf16[2,128,1024]{2,1,0:T(8,128)(2,1)}, u32[]{:S(2)}) copy-start(bf16[2,128,1024]{2,1,0:T(8,128)(2,1)} %param.16) | copy-start | bytes 1572868
  328.3 106.9 %copy-start.13 = (bf16[2,128,1024]{2,1,0:T(8,128)(2,1)}, bf16[2,128,1024]{2,1,0:T(8,128)(2,1)S(1)}, u32[]{:S(2)}) copy-start(bf16[2,128,1024]{2,1,0:T(8,128)(2,1)S(1)} %get-tuple-element.432) | copy-start | bytes 1572868
  350.8 257.7 %copy-start.7 = (f32[256,1024]{1,0:T(8,128)}, f32[256,1024]{1,0:T(8,128)S(1)}, u32[]{:S(2)}) copy-start(f32[256,1024]{1,0:T(8,128)S(1)} %get-tuple-element.616) | copy-start | bytes 3145732
  351.0 155.6 %copy-start.10 = (bf16[256,1024]{1,0:T(8,128)(2,1)}, bf16[256,1024]{1,0:T(8,128)(2,1)S(1)}, u32[]{:S(2)}) copy-start(bf16[256,1024]{1,0:T(8,128)(2,1)S(1)} %multiply_convert_fusion.5) | copy-start | bytes 1572868
  435.2 150.3 %copy-start.19 = (bf16[2,128,1024]{2,1,0:T(8,128)(2,1)S(1)}, bf16[2,128,1024]{2,1,0:T(8,128)(2,1)}, u32[]{:S(2)}) copy-start(bf16[2,128,1024]{2,1,0:T(8,128)(2,1)} %param.27) | copy-start | bytes 1572868
  598.5 7.3 copy-start.22
  598.5 7.3 copy-start.21
  598.5 7.3 copy-start.26
  605.8 4.0 copy-start.9
  618.3 4.8 copy-start.1
  630.8 4.8 copy-start.1
  643.3 4.8 copy-start.1
  655.8 4.8 copy-start.1
  668.2 4.8 copy-start.1
  680.6 4.8 copy-start.1
  693.1 4.8 copy-start.1
  705.6 4.8 copy-start.1
  717.0 178.4 %reduce-scatter.12.cloned.1.call-start = ((), (), s32[]{:S(2)}) async-start(), calls=%async_computation.18 | async-start | bytes 4718592 | tf_op jit(solution)/shard_map/reduce_scatter | solution.py:261
  717.6 324.4 %reduce-scatter.14.cloned.1.call-start = ((), (), s32[]{:S(2)}) async-start(), calls=%async_computation.19 | async-start | bytes 4325376 | tf_op jit(solution)/shard_map/reduce_scatter | solution.py:282
  718.1 2.9 copy-start.6
  718.1 2.9 copy-start.14
  721.0 463.9 %reduce-scatter.20.cloned.1.call-start = ((), (), s32[]{:S(2)}) async-start(), calls=%async_computation.22 | async-start | bytes 4325376 | tf_op jit(solution)/shard_map/reduce_scatter | solution.py:285
  723.8 605.0 %reduce-scatter.16.cloned.1.call-start = ((), (), s32[]{:S(2)}) async-start(), calls=%async_computation.20 | async-start | bytes 4325376 | tf_op jit(solution)/shard_map/reduce_scatter | solution.py:283
  807.6 91.7 %copy-start.11 = (bf16[256,1024]{1,0:T(8,128)(2,1)S(1)}, bf16[256,1024]{1,0:T(8,128)(2,1)}, u32[]{:S(2)}) copy-start(bf16[256,1024]{1,0:T(8,128)(2,1)} %copy-done.10) | copy-start | bytes 1572868
  807.6 664.9 %reduce-scatter.18.cloned.1.call-start = ((), (), s32[]{:S(2)}) async-start(), calls=%async_computation.21 | async-start | bytes 4325376 | tf_op jit(solution)/shard_map/reduce_scatter | solution.py:284
  899.2 932.2 %reduce-scatter.22.cloned.1.call-start = ((), (), s32[]{:S(2)}) async-start(), calls=%async_computation.23 | async-start | bytes 17301504 | tf_op jit(solution)/shard_map/reduce_scatter | solution.py:287
  909.1 1282.4 %reduce-scatter.24.cloned.1.call-start = ((), (), s32[]{:S(2)}) async-start(), calls=%async_computation.24 | async-start | bytes 17301504 | tf_op jit(solution)/shard_map/reduce_scatter | solution.py:288
  918.8 1632.7 %reduce-scatter.26.cloned.1.call-start = ((), (), s32[]{:S(2)}) async-start(), calls=%async_computation.25 | async-start | bytes 17301504 | tf_op jit(solution)/shard_map/reduce_scatter | solution.py:289
  929.6 2.5 copy-start.8
  932.0 7.3 copy-start.15
  932.1 7.3 copy-start.17
  (24 other events, 31.7 us)
Sparse Core Ops, SparseCore 0:
  11.0 59.2 all-gather.12
  73.3 55.3 all-gather.8
  131.7 71.2 all-gather.10
  205.4 85.3 all-gather.14
  293.6 54.7 all-gather.16
  351.2 76.2 all-gather.18
  430.5 75.9 all-gather.20
  509.5 75.9 all-gather.22
  717.1 86.6 reduce-scatter.9
  807.7 87.6 reduce-scatter.11
  898.2 143.6 reduce-scatter.13
  1044.6 140.1 reduce-scatter.19
  1187.7 141.0 reduce-scatter.15
  1331.5 141.0 reduce-scatter.17
  1475.3 356.1 reduce-scatter.21
  1834.2 357.2 reduce-scatter.23
  2194.2 357.3 reduce-scatter.25
